TPU v7x, 32 devices: a whole 2x2x4 slice. The times are simulated.
32 devices in a mesh: lon: 8 (over z, y), rad: 4 (over x, core).
Axes of the slice: x: 2, y: 2, z: 4, core: 2. Of those that a mesh axis runs over, the one named last changes fastest.
Arguments:
- adjoint_temp: float32 [32, 256, 128], P('rad', 'lon'), may hold values from -6 to 6
- viscosity: float32 [32, 256, 128], P('rad', 'lon'), may hold values from 0.1 to 10
- velocity: float32 [3, 32, 256, 128], P(None, 'rad', 'lon'), may hold values from -6 to 6
- misfit_force: float32 [3, 32, 256, 128], P(None, 'rad', 'lon'), may hold values from -6 to 6
- adjoint_guess: float32 [3, 32, 256, 128], P(None, 'rad', 'lon'), may hold values from -3 to 3
Outputs:
- temp_next: float32 [32, 256, 128], P('rad', 'lon')
- adjoint_vel: float32 [3, 32, 256, 128], P(None, 'rad', 'lon')
All inputs are finite; a program needn't handle non-finite values.
Results may differ from a plain program's by a relative error of at most 0.00002.
Values sent between devices are 32-bit elements; how exact they have to be, the bound alone decides.
A program may use at most 128 MiB of HBM per device.

v0:
```python
import functools

import jax
import jax.numpy as jnp
from jax import lax
from jax.experimental import pallas as pl
from jax.experimental.pallas import tpu as pltpu
from jax.sharding import PartitionSpec as P

NU = 2
NC = 8
PAD = 8
MESH = pl.DeviceIdType.MESH


def kernel(ni, nj, temp_ref, visc_ref, vel_ref, mis_ref, guess_ref, tn_ref, out_ref,
           W0, U1, U2, U3, U4, WT, B, D, RS, CP, CV, G, CG, CW, CB, EA, EB, EX,
           S0, L0, S, L, send, recv):
    R, C, LAT = temp_ref.shape
    half = R // 4
    cols = C // 2
    strip = PAD
    i = lax.axis_index("lon")
    j = lax.axis_index("rad")
    west, east = lax.rem(i + ni - 1, ni), lax.rem(i + 1, ni)
    down, up = lax.rem(j + nj - 1, nj), lax.rem(j + 1, nj)

    barrier = pltpu.get_barrier_semaphore()
    for d in range(nj):
        other = lax.rem(j + d, nj)
        for lon in (west, east) if d == 0 else (west, east, i):
            pl.semaphore_signal(barrier, inc=1, device_id={"lon": lon, "rad": other}, device_id_type=MESH)

    mid = pl.ds(PAD, C)
    lane = lax.broadcasted_iota(jnp.int32, (C, LAT), 1)
    first, last = lane == 0, lane == LAT - 1
    even = lax.rem(lane, 2) == 0
    even_half = even[:cols]

    W0[0:3, 1 : R + 1, PAD : PAD + C, :] = guess_ref[...]
    W0[3, 1 : R + 1, PAD : PAD + C, :] = temp_ref[...]
    W0[4, 1 : R + 1, PAD : PAD + C, :] = visc_ref[...]

    def pack(slot, dst):
        for r in range(half):
            a = RS[slot, r, pl.ds(0, cols, 2), :] + RS[slot, r, pl.ds(1, cols, 2), :]
            b = RS[slot, r + half, pl.ds(0, cols, 2), :] + RS[slot, r + half, pl.ds(1, cols, 2), :]
            a = a + pltpu.roll(a, LAT - 1, 1)
            b = b + pltpu.roll(b, 1, 1)
            dst[r] = 0.125 * jnp.where(even_half, a, b)

    for q in range(2 * half):
        RS[3, q] = visc_ref[2 * q] + visc_ref[2 * q + 1]
    pack(3, CV.at[0])

    def copy(src, dst, slot, lon, rad):
        return pltpu.make_async_remote_copy(
            src_ref=src, dst_ref=dst, send_sem=send.at[slot], recv_sem=recv.at[slot],
            device_id={"lon": lon, "rad": rad}, device_id_type=MESH)

    pending = []

    def begin(slot, buf, stage, land, comps):
        for c in range(comps):
            stage[0, c] = buf[c, 1 : R + 1, PAD, :]
            stage[1, c] = buf[c, 1 : R + 1, PAD + C - 1, :]
        copies = [
            copy(stage.at[0], land.at[1], slot, west, j),
            copy(stage.at[1], land.at[0], slot + 1, east, j),
            copy(buf.at[:, 1, mid], buf.at[:, R + 1, mid], slot + 2, i, down),
            copy(buf.at[:, R, mid], buf.at[:, 0, mid], slot + 3, i, up),
        ]
        for item in copies:
            item.start()
        pending.extend(copies)
        return copies

    def finish(copies, buf, land, comps):
        for item in copies:
            item.wait_recv()
        for c in range(comps):
            buf[c, 1 : R + 1, PAD - 1, :] = land[0, c]
            buf[c, 1 : R + 1, PAD + C, :] = land[1, c]

    gathers = 3 * nj - 1

    def gather(slot, src, dst, width):
        copies = []
        rows = pl.ds(1 + half * j, half)
        for d in range(nj):
            other = lax.rem(j + d, nj)
            copies.append(copy(src.at[:, :, pl.ds(0, width)], dst.at[:, rows, pl.ds(2 * strip + cols, width)], slot, west, other))
            copies.append(copy(src.at[:, :, pl.ds(cols - width, width)], dst.at[:, rows, pl.ds(2 * strip - width, width)], slot + 1, east, other))
            slot = slot + 2
            if d > 0:
                copies.append(copy(src, dst.at[:, rows, pl.ds(2 * strip, cols)], slot, i, other))
                slot = slot + 1
        for item in copies:
            item.start()
        pending.extend(copies)
        for r in range(half):
            dst[:, 1 + half * j + r, 2 * strip : 2 * strip + cols, :] = src[:, r]
        return copies

    top = half * nj + 1
    for buf in (EA, EB):
        buf[...] = jnp.zeros_like(buf)
    CG[0, 0] = jnp.zeros_like(CG[0, 0])
    CG[0, top] = jnp.zeros_like(CG[0, top])

    pl.semaphore_wait(barrier, gathers)

    round0 = begin(0, W0, S0, L0, 5)
    coarse_visc = gather(16, CV, CG, cols)
    finish(round0, W0, L0, 5)

    @pl.when(j == 0)
    def _():
        W0[3:5, 0] = jnp.zeros_like(W0[3:5, 0])

    @pl.when(j == nj - 1)
    def _():
        W0[3:5, R + 1] = jnp.zeros_like(W0[3:5, R + 1])

    def near(buf, c, r):
        x = buf[c, r + 1, PAD : PAD + C, :]
        return x, [
            buf[c, r + 1, PAD - 1 : PAD + C - 1, :],
            buf[c, r + 1, PAD + 1 : PAD + C + 1, :],
            buf[c, r, PAD : PAD + C, :],
            buf[c, r + 2, PAD : PAD + C, :],
            pltpu.roll(x, 1, 1),
            pltpu.roll(x, LAT - 1, 1),
        ]

    def setup(r, carry):
        v, vn = near(W0, 4, r)
        vn[4] = jnp.where(first, 0.0, vn[4])
        vn[5] = jnp.where(last, 0.0, vn[5])
        coefs = [(v + item) * 0.5 for item in vn]
        diag = coefs[0] + coefs[1] + coefs[2] + coefs[3] + coefs[4] + coefs[5]
        inv = 0.8 / diag
        coefs[4] = jnp.where(first, 0.0, coefs[4])
        coefs[5] = jnp.where(last, 0.0, coefs[5])
        for k in range(6):
            WT[k, r] = coefs[k] * inv
        D[r] = diag * 1.25
        t, tn = near(W0, 3, r)
        tn[4] = jnp.where(first, 0.0, tn[4])
        tn[5] = jnp.where(last, 0.0, tn[5])
        advect = vel_ref[0, r] * (tn[3] - tn[2]) + vel_ref[1, r] * (tn[1] - tn[0]) + vel_ref[2, r] * (tn[5] - tn[4])
        spread = tn[0] + tn[1] + tn[2] + tn[3] + tn[4] + tn[5] - 6.0 * t
        t_next = t + 0.125 * advect + 0.1 * spread
        tn_ref[r] = t_next
        B[0, r] = (mis_ref[0, r] + t_next) * inv
        B[1, r] = mis_ref[1, r] * inv
        B[2, r] = mis_ref[2, r] * inv
        return carry

    lax.fori_loop(0, R, setup, 0)

    @pl.when(j == 0)
    def _():
        WT[2, 0] = jnp.zeros_like(WT[2, 0])

    @pl.when(j == nj - 1)
    def _():
        WT[3, R - 1] = jnp.zeros_like(WT[3, R - 1])

    def change(buf, c, r):
        x, xn = near(buf, c, r)
        t = B[c, r] - 0.8 * x
        for k in range(6):
            t = t + WT[k, r] * xn[k]
        return x, t

    def sweep(src, dst):
        def body(r, carry):
            for c in range(3):
                x, t = change(src, c, r)
                dst[c, r + 1, PAD : PAD + C, :] = x + t
            return carry

        lax.fori_loop(0, R, body, 0)

    sweep(W0, U1)
    round1 = begin(4, U1, S.at[0], L.at[0], 3)

    for item in coarse_visc:
        item.wait_recv()

    def coarse_near(buf, c, at, r):
        p = 1 + half * at + r
        x = buf[c, p, PAD : PAD + C, :]
        if r > 0:
            below = buf[c, p - 1, PAD : PAD + C, :]
        else:
            below = jnp.where(even, pltpu.roll(buf[c, p - 1, PAD : PAD + C, :], LAT - 1, 1),
                              pltpu.roll(buf[c, p + half - 1, PAD : PAD + C, :], 1, 1))
        if r < half - 1:
            above = buf[c, p + 1, PAD : PAD + C, :]
        else:
            above = jnp.where(even, pltpu.roll(buf[c, p - half + 1, PAD : PAD + C, :], LAT - 1, 1),
                              pltpu.roll(buf[c, p + 1, PAD : PAD + C, :], 1, 1))
        return x, [
            buf[c, p, PAD - 1 : PAD + C - 1, :],
            buf[c, p, PAD + 1 : PAD + C + 1, :],
            below,
            above,
            pltpu.roll(x, 2, 1),
            pltpu.roll(x, LAT - 2, 1),
        ]

    def coarse_setup(at, carry):
        for r in range(half):
            v, vn = coarse_near(CG, 0, at, r)
            vn[4] = jnp.where(lane < 2, 0.0, vn[4])
            vn[5] = jnp.where(lane >= LAT - 2, 0.0, vn[5])
            coefs = [(v + item) * 0.5 for item in vn]
            diag = coefs[0] + coefs[1] + coefs[2] + coefs[3] + coefs[4] + coefs[5]
            inv = 0.8 / diag
            coefs[4] = jnp.where(lane < 2, 0.0, coefs[4])
            coefs[5] = jnp.where(lane >= LAT - 2, 0.0, coefs[5])
            for k in range(6):
                CW[k, half * at + r] = coefs[k] * inv
            CW[6, half * at + r] = 4.0 * inv
        return carry

    lax.fori_loop(0, nj, coarse_setup, 0)

    finish(round1, U1, L.at[0], 3)
    sweep(U1, U2)
    round2 = begin(8, U2, S.at[1], L.at[1], 3)
    finish(round2, U2, L.at[1], 3)

    def residual(q, carry):
        for c in range(3):
            total = D[2 * q] * change(U2, c, 2 * q)[1]
            RS[c, q] = total + D[2 * q + 1] * change(U2, c, 2 * q + 1)[1]
        return carry

    lax.fori_loop(0, 2 * half, residual, 0)
    for c in range(3):
        pack(c, CP.at[c])
    coarse_res = gather(16 + gathers, CP, G, strip)
    for item in coarse_res:
        item.wait_recv()

    def coarse_first(p, carry):
        for c in range(3):
            b = G[c, p + 1, PAD : PAD + C, :] * CW[6, p]
            CB[c, p] = b
            EA[c, p + 1, PAD : PAD + C, :] = b
        return carry

    lax.fori_loop(0, half * nj, coarse_first, 0)

    def coarse_sweep(src, dst):
        def body(at, carry):
            for r in range(half):
                p = half * at + r
                for c in range(3):
                    x, xn = coarse_near(src, c, at, r)
                    t = CB[c, p] + 0.2 * x
                    for k in range(6):
                        t = t + CW[k, p] * xn[k]
                    dst[c, p + 1, PAD : PAD + C, :] = t
            return carry

        lax.fori_loop(0, nj, body, 0)

    src, dst = EA, EB
    for number in range(NC - 1):
        coarse_sweep(src, dst)
        src, dst = dst, src

    wide = EX.shape[2] // 2
    start = 2 * strip - PAD // 2
    even_wide = lax.rem(lax.broadcasted_iota(jnp.int32, (wide, LAT), 1), 2) == 0
    for c in range(3):
        for q in range(-1, 2 * half + 1):
            low = 0 <= q < half or q == 2 * half
            place = 1 + half * j + {-1: -1, 2 * half: half}.get(q, q % half)
            x = src[c, place, start : start + wide, :]
            if low:
                x = jnp.where(even_wide, x, pltpu.roll(x, 1, 1))
            else:
                x = jnp.where(even_wide, pltpu.roll(x, LAT - 1, 1), x)
            EX[c, q + 1, pl.ds(0, wide, 2), :] = x
            EX[c, q + 1, pl.ds(1, wide, 2), :] = x
    for c in range(3):
        for r in range(-1, R + 1):
            U3[c, r + 1] = U2[c, r + 1] + EX[c, r // 2 + 1]

    sweep(U3, U4)
    round3 = begin(12, U4, S.at[2], L.at[2], 3)
    finish(round3, U4, L.at[2], 3)

    def closing(r, carry):
        for c in range(3):
            x, t = change(U4, c, r)
            out_ref[c, r] = x + t
        return carry

    lax.fori_loop(0, R, closing, 0)
    for item in pending:
        item.wait_send()


def solution(mesh):
    ni, nj = mesh.shape["lon"], mesh.shape["rad"]

    def local(adjoint_temp, viscosity, velocity, misfit_force, adjoint_guess):
        R, C, LAT = adjoint_temp.shape
        half, cols, wide = R // 4, C // 2, C + 2 * PAD
        f32 = jnp.float32
        frame = lambda n, rows: pltpu.VMEM((n, rows, wide, LAT), f32)
        block = lambda *dims: pltpu.VMEM(dims + (C, LAT), f32)
        copies = 16 + 2 * (3 * nj - 1)
        vmem = pl.BlockSpec(memory_space=pltpu.VMEM)
        P8 = half * nj
        return pl.pallas_call(
            functools.partial(kernel, ni, nj),
            out_shape=(
                jax.ShapeDtypeStruct(adjoint_temp.shape, f32),
                jax.ShapeDtypeStruct(adjoint_guess.shape, f32),
            ),
            in_specs=[vmem] * 5,
            out_specs=(vmem, vmem),
            scratch_shapes=[
                frame(5, R + 2), frame(3, R + 2), frame(3, R + 2), frame(3, R + 2), frame(3, R + 2),
                block(6, R), block(3, R), block(R), block(4, 2 * half),
                pltpu.VMEM((3, half, cols, LAT), f32), pltpu.VMEM((1, half, cols, LAT), f32),
                frame(3, P8 + 2), frame(1, P8 + 2), block(7, P8), block(3, P8),
                frame(3, P8 + 2), frame(3, P8 + 2), frame(3, 2 * half + 2),
                pltpu.VMEM((2, 5, R, LAT), f32), pltpu.VMEM((2, 5, R, LAT), f32),
                pltpu.VMEM((3, 2, 3, R, LAT), f32), pltpu.VMEM((3, 2, 3, R, LAT), f32),
                pltpu.SemaphoreType.DMA((copies,)), pltpu.SemaphoreType.DMA((copies,)),
            ],
            compiler_params=pltpu.CompilerParams(collective_id=0, has_side_effects=True),
        )(adjoint_temp, viscosity, velocity, misfit_force, adjoint_guess)

    flat = P("rad", "lon", None)
    full = P(None, "rad", "lon", None)
    return jax.shard_map(local, mesh=mesh, in_specs=(flat, flat, full, full, full), out_specs=(flat, full), check_vma=False)
```

profile of v0, /device:TPU:1, one launch (start us, length us, event | category | flops | bytes accessed | tf_op | source)
XLA Modules:
  0.0 44.2 jit_solution(5282125501489225889)
XLA Ops:
  0.6 40.2 %shard_map.68 = (f32[8,32,128]{2,1,0:T(8,128)}, f32[3,8,32,128]{3,2,1,0:T(8,128)}) custom-call(f32[8,32,128]{2,1,0:T(8,128)} %temp_ref.1, f32[8,32,128]{2,1,0:T(8,128)} %visc_ref.1, f32[3,8,32,128]{3,2,1,0:T(8,128)} %vel_ref.1, f32[3,8,32,128]{3,2,1,0:T(8,128)} %mis_ref.1, f32[3,8,32,128]{3,2,1,0:T(8,128)} %guess_ref.1), custom_call_target="tpu_custom_call" | custom-call | tf_op jit(solution)/shard_map/pallas_call | solution.py:322
  40.9 1.6 %copy.9 = f32[8,32,128]{2,1,0:T(8,128)} copy(f32[8,32,128]{2,1,0:T(8,128)} %get-tuple-element.4) | data formatting | bytes 262144
  42.4 1.8 %copy.10 = f32[3,8,32,128]{3,2,1,0:T(8,128)} copy(f32[3,8,32,128]{3,2,1,0:T(8,128)} %get-tuple-element.5) | data formatting | bytes 786432
where the time goes:
time: 45 us; the launch traced here: 44.2 us
  Pallas kernels  40.2 us (89%)
  local copies, waits for them, and re-layouts  3.33 us (7%)
  between operations  0.64 us (1%)
    pallas_call x1, Pallas kernels, local(): pl.pallas_call(functools.partial(kernel, ni, nj), out_shape=(jax.ShapeDty...  40.2 us
    unnamed x2, local copies, waits for them, and re-layouts  3.33 us

commit v1 on v0

--- a/solution.py
+++ b/solution.py
@@ -13,10 +13,11 @@
 MESH = pl.DeviceIdType.MESH
 
 
-def kernel(ni, nj, temp_ref, visc_ref, vel_ref, mis_ref, guess_ref, tn_ref, out_ref,
+def kernel(ni, nj, temp_hbm, visc_hbm, vel_hbm, mis_hbm, guess_hbm, tn_ref, out_ref,
+           vel_ref, mis_ref, local,
            W0, U1, U2, U3, U4, WT, B, D, RS, CP, CV, G, CG, CW, CB, EA, EB, EX,
            S0, L0, S, L, send, recv):
-    R, C, LAT = temp_ref.shape
+    R, C, LAT = temp_hbm.shape
     half = R // 4
     cols = C // 2
     strip = PAD
@@ -25,21 +26,28 @@
     west, east = lax.rem(i + ni - 1, ni), lax.rem(i + 1, ni)
     down, up = lax.rem(j + nj - 1, nj), lax.rem(j + 1, nj)
 
+    mid = pl.ds(PAD, C)
+    inner = pl.ds(1, R)
+    loads = [
+        pltpu.make_async_copy(visc_hbm, W0.at[4, inner, mid], local.at[0]),
+        pltpu.make_async_copy(temp_hbm, W0.at[3, inner, mid], local.at[1]),
+        pltpu.make_async_copy(guess_hbm, W0.at[0:3, inner, mid], local.at[2]),
+        pltpu.make_async_copy(vel_hbm, vel_ref, local.at[3]),
+        pltpu.make_async_copy(mis_hbm, mis_ref, local.at[4]),
+    ]
+    for item in loads:
+        item.start()
+
     barrier = pltpu.get_barrier_semaphore()
     for d in range(nj):
         other = lax.rem(j + d, nj)
         for lon in (west, east) if d == 0 else (west, east, i):
             pl.semaphore_signal(barrier, inc=1, device_id={"lon": lon, "rad": other}, device_id_type=MESH)
 
-    mid = pl.ds(PAD, C)
     lane = lax.broadcasted_iota(jnp.int32, (C, LAT), 1)
     first, last = lane == 0, lane == LAT - 1
     even = lax.rem(lane, 2) == 0
     even_half = even[:cols]
-
-    W0[0:3, 1 : R + 1, PAD : PAD + C, :] = guess_ref[...]
-    W0[3, 1 : R + 1, PAD : PAD + C, :] = temp_ref[...]
-    W0[4, 1 : R + 1, PAD : PAD + C, :] = visc_ref[...]
 
     def pack(slot, dst):
         for r in range(half):
@@ -49,9 +57,6 @@
             b = b + pltpu.roll(b, 1, 1)
             dst[r] = 0.125 * jnp.where(even_half, a, b)
 
-    for q in range(2 * half):
-        RS[3, q] = visc_ref[2 * q] + visc_ref[2 * q + 1]
-    pack(3, CV.at[0])
 
     def copy(src, dst, slot, lon, rad):
         return pltpu.make_async_remote_copy(
@@ -108,10 +113,18 @@
     CG[0, 0] = jnp.zeros_like(CG[0, 0])
     CG[0, top] = jnp.zeros_like(CG[0, top])
 
+    loads[0].wait()
+    for q in range(2 * half):
+        RS[3, q] = W0[4, 2 * q + 1, PAD : PAD + C, :] + W0[4, 2 * q + 2, PAD : PAD + C, :]
+    pack(3, CV.at[0])
+    loads[1].wait()
+    loads[2].wait()
     pl.semaphore_wait(barrier, gathers)
 
     round0 = begin(0, W0, S0, L0, 5)
     coarse_visc = gather(16, CV, CG, cols)
+    loads[3].wait()
+    loads[4].wait()
     finish(round0, W0, L0, 5)
 
     @pl.when(j == 0)
@@ -189,27 +202,21 @@
     for item in coarse_visc:
         item.wait_recv()
 
-    def coarse_near(buf, c, at, r):
+    def coarse_near(buf, c, at, r, lo=PAD, width=None):
+        width = width or C
+        part = even[:width]
         p = 1 + half * at + r
-        x = buf[c, p, PAD : PAD + C, :]
+        block = lambda place, off=0: buf[c, place, lo + off : lo + off + width, :]
+        x = block(p)
         if r > 0:
-            below = buf[c, p - 1, PAD : PAD + C, :]
+            below = block(p - 1)
         else:
-            below = jnp.where(even, pltpu.roll(buf[c, p - 1, PAD : PAD + C, :], LAT - 1, 1),
-                              pltpu.roll(buf[c, p + half - 1, PAD : PAD + C, :], 1, 1))
+            below = jnp.where(part, pltpu.roll(block(p - 1), LAT - 1, 1), pltpu.roll(block(p + half - 1), 1, 1))
         if r < half - 1:
-            above = buf[c, p + 1, PAD : PAD + C, :]
+            above = block(p + 1)
         else:
-            above = jnp.where(even, pltpu.roll(buf[c, p - half + 1, PAD : PAD + C, :], LAT - 1, 1),
-                              pltpu.roll(buf[c, p + 1, PAD : PAD + C, :], 1, 1))
-        return x, [
-            buf[c, p, PAD - 1 : PAD + C - 1, :],
-            buf[c, p, PAD + 1 : PAD + C + 1, :],
-            below,
-            above,
-            pltpu.roll(x, 2, 1),
-            pltpu.roll(x, LAT - 2, 1),
-        ]
+            above = jnp.where(part, pltpu.roll(block(p - half + 1), LAT - 1, 1), pltpu.roll(block(p + 1), 1, 1))
+        return x, [block(p, -1), block(p, 1), below, above, pltpu.roll(x, 2, 1), pltpu.roll(x, LAT - 2, 1)]
 
     def coarse_setup(at, carry):
         for r in range(half):
@@ -255,23 +262,28 @@
 
     lax.fori_loop(0, half * nj, coarse_first, 0)
 
-    def coarse_sweep(src, dst):
+    def coarse_sweep(src, dst, rim):
+        near_rim = 2 * rim <= PAD and cols % 8 == 0
+        lo = 2 * strip - PAD // 2 if near_rim else PAD
+        width = cols + PAD if near_rim else C
+        reach = -(-rim // (2 * half))
+
         def body(at, carry):
             for r in range(half):
                 p = half * at + r
                 for c in range(3):
-                    x, xn = coarse_near(src, c, at, r)
-                    t = CB[c, p] + 0.2 * x
+                    x, xn = coarse_near(src, c, at, r, lo, width)
+                    t = CB[c, p, lo - PAD : lo - PAD + width, :] + 0.2 * x
                     for k in range(6):
-                        t = t + CW[k, p] * xn[k]
-                    dst[c, p + 1, PAD : PAD + C, :] = t
+                        t = t + CW[k, p, lo - PAD : lo - PAD + width, :] * xn[k]
+                    dst[c, p + 1, lo : lo + width, :] = t
             return carry
 
-        lax.fori_loop(0, nj, body, 0)
+        lax.fori_loop(jnp.maximum(j - reach, 0), jnp.minimum(j + reach + 1, nj), body, 0)
 
     src, dst = EA, EB
     for number in range(NC - 1):
-        coarse_sweep(src, dst)
+        coarse_sweep(src, dst, NC - 1 - number)
         src, dst = dst, src
 
     wide = EX.shape[2] // 2
@@ -307,6 +319,14 @@
         item.wait_send()
 
 
+def deliver(tn_ref, out_ref, tn_hbm, out_hbm, sems):
+    copies = [pltpu.make_async_copy(tn_ref, tn_hbm, sems.at[0]), pltpu.make_async_copy(out_ref, out_hbm, sems.at[1])]
+    for item in copies:
+        item.start()
+    for item in copies:
+        item.wait()
+
+
 def solution(mesh):
     ni, nj = mesh.shape["lon"], mesh.shape["rad"]
 
@@ -317,17 +337,18 @@
         frame = lambda n, rows: pltpu.VMEM((n, rows, wide, LAT), f32)
         block = lambda *dims: pltpu.VMEM(dims + (C, LAT), f32)
         copies = 16 + 2 * (3 * nj - 1)
-        vmem = pl.BlockSpec(memory_space=pltpu.VMEM)
+        vmem, place = pl.BlockSpec(memory_space=pltpu.VMEM), pl.BlockSpec(memory_space=pl.ANY)
         P8 = half * nj
-        return pl.pallas_call(
+        results = pl.pallas_call(
             functools.partial(kernel, ni, nj),
             out_shape=(
-                jax.ShapeDtypeStruct(adjoint_temp.shape, f32),
-                jax.ShapeDtypeStruct(adjoint_guess.shape, f32),
+                pltpu.VMEM(adjoint_temp.shape, f32),
+                pltpu.VMEM(adjoint_guess.shape, f32),
             ),
-            in_specs=[vmem] * 5,
+            in_specs=[place] * 5,
             out_specs=(vmem, vmem),
             scratch_shapes=[
+                block(3, R), block(3, R), pltpu.SemaphoreType.DMA((5,)),
                 frame(5, R + 2), frame(3, R + 2), frame(3, R + 2), frame(3, R + 2), frame(3, R + 2),
                 block(6, R), block(3, R), block(R), block(4, 2 * half),
                 pltpu.VMEM((3, half, cols, LAT), f32), pltpu.VMEM((1, half, cols, LAT), f32),
@@ -339,6 +360,13 @@
             ],
             compiler_params=pltpu.CompilerParams(collective_id=0, has_side_effects=True),
         )(adjoint_temp, viscosity, velocity, misfit_force, adjoint_guess)
+        return pl.pallas_call(
+            deliver,
+            out_shape=(jax.ShapeDtypeStruct(adjoint_temp.shape, f32), jax.ShapeDtypeStruct(adjoint_guess.shape, f32)),
+            in_specs=[vmem] * 2,
+            out_specs=(place, place),
+            scratch_shapes=[pltpu.SemaphoreType.DMA((2,))],
+        )(*[pltpu.with_memory_space_constraint(item, pltpu.VMEM) for item in results])
 
     flat = P("rad", "lon", None)
     full = P(None, "rad", "lon", None)

time: 45 us -> 38.5 us (0.86); the launches traced: 44.2 us -> 38.4 us
  local copies, waits for them, and re-layouts: 3.33 us -> 0 us
  Pallas kernels: 40.2 us -> 37.7 us
    unnamed x2 -> x0, local copies, waits for them, and re-layouts: 3.33 us -> none
    pallas_call x1 -> x2, Pallas kernels: 40.2 us -> 37.7 us  [the longest x1 36.9 us: local(): pl.pallas_call(functools.partial(kernel, ni, nj), out_shape=(pltpu.VMEM(a...]
where the time goes in v1:
time: 38.5 us; the launch traced here: 38.4 us
  Pallas kernels  37.7 us (98%)
  between operations  0.64 us (2%)
    pallas_call x1, Pallas kernels, local(): pl.pallas_call(functools.partial(kernel, ni, nj), out_shape=(pltpu.VMEM(a...  36.9 us
    pallas_call x1, Pallas kernels, local(): pl.pallas_call(deliver, out_shape=(jax.ShapeDtypeStruct(adjoint_temp.shap...  0.81 us

profile of v1, /device:TPU:1, one launch (start us, length us, event | category | flops | bytes accessed | tf_op | source)
XLA Modules:
  0.0 38.4 jit_solution(9914235344617587372)
XLA Ops:
  0.6 36.9 %shard_map.68 = (f32[8,32,128]{2,1,0:T(8,128)S(1)}, f32[3,8,32,128]{3,2,1,0:T(8,128)S(1)}) custom-call(f32[8,32,128]{2,1,0:T(8,128)} %temp_hbm.1, f32[8,32,128]{2,1,0:T(8,128)} %visc_hbm.1, f32[3,8,32,128]{3,2,1,0:T(8,128)} %vel_hbm.1, f32[3,8,32,128]{3,2,1,0:T(8,128)} %mis_hbm.1, f32[3,8,32,128]{3,2,1,0:T(8,128)} %guess_hbm.1), custom_call_target="tpu_custom_call" | custom-call | tf_op jit(solution)/shard_map/pallas_call | solution.py:342
  37.6 0.8 %shard_map.69 = (f32[8,32,128]{2,1,0:T(8,128)}, f32[3,8,32,128]{3,2,1,0:T(8,128)}) custom-call(f32[8,32,128]{2,1,0:T(8,128)S(1)} %get-tuple-element.4.tn_ref, f32[3,8,32,128]{3,2,1,0:T(8,128)S(1)} %get-tuple-element.5.out_ref), custom_call_target="tpu_custom_call" | custom-call | tf_op jit(solution)/shard_map/pallas_call | solution.py:363

commit v2 on v1

--- a/solution.py
+++ b/solution.py
@@ -15,7 +15,7 @@
 
 def kernel(ni, nj, temp_hbm, visc_hbm, vel_hbm, mis_hbm, guess_hbm, tn_ref, out_ref,
            vel_ref, mis_ref, local,
-           W0, U1, U2, U3, U4, WT, B, D, RS, CP, CV, G, CG, CW, CB, EA, EB, EX,
+           W0, U1, U2, U3, U4, SW, LW, WT, B, D, RS, CP, CV, G, CG, CW, CB, EA, EB, EX,
            S0, L0, S, L, send, recv):
     R, C, LAT = temp_hbm.shape
     half = R // 4
@@ -122,7 +122,7 @@
     pl.semaphore_wait(barrier, gathers)
 
     round0 = begin(0, W0, S0, L0, 5)
-    coarse_visc = gather(16, CV, CG, cols)
+    coarse_visc = gather(20, CV, CG, cols)
     loads[3].wait()
     loads[4].wait()
     finish(round0, W0, L0, 5)
@@ -156,7 +156,7 @@
         coefs[4] = jnp.where(first, 0.0, coefs[4])
         coefs[5] = jnp.where(last, 0.0, coefs[5])
         for k in range(6):
-            WT[k, r] = coefs[k] * inv
+            WT[k, r + 1, PAD : PAD + C, :] = coefs[k] * inv
         D[r] = diag * 1.25
         t, tn = near(W0, 3, r)
         tn[4] = jnp.where(first, 0.0, tn[4])
@@ -174,17 +174,17 @@
 
     @pl.when(j == 0)
     def _():
-        WT[2, 0] = jnp.zeros_like(WT[2, 0])
+        WT[2, 1] = jnp.zeros_like(WT[2, 1])
 
     @pl.when(j == nj - 1)
     def _():
-        WT[3, R - 1] = jnp.zeros_like(WT[3, R - 1])
+        WT[3, R] = jnp.zeros_like(WT[3, R])
 
     def change(buf, c, r):
         x, xn = near(buf, c, r)
         t = B[c, r] - 0.8 * x
         for k in range(6):
-            t = t + WT[k, r] * xn[k]
+            t = t + WT[k, r + 1, PAD : PAD + C, :] * xn[k]
         return x, t
 
     def sweep(src, dst):
@@ -198,6 +198,7 @@
 
     sweep(W0, U1)
     round1 = begin(4, U1, S.at[0], L.at[0], 3)
+    round_w = begin(16, WT, SW, LW, 6)
 
     for item in coarse_visc:
         item.wait_recv()
@@ -242,14 +243,18 @@
 
     def residual(q, carry):
         for c in range(3):
-            total = D[2 * q] * change(U2, c, 2 * q)[1]
-            RS[c, q] = total + D[2 * q + 1] * change(U2, c, 2 * q + 1)[1]
+            x, t = change(U2, c, 2 * q)
+            U3[c, 2 * q + 1, PAD : PAD + C, :] = x + t
+            x, s = change(U2, c, 2 * q + 1)
+            U3[c, 2 * q + 2, PAD : PAD + C, :] = x + s
+            RS[c, q] = D[2 * q] * t + D[2 * q + 1] * s
         return carry
 
     lax.fori_loop(0, 2 * half, residual, 0)
     for c in range(3):
         pack(c, CP.at[c])
-    coarse_res = gather(16 + gathers, CP, G, strip)
+    coarse_res = gather(20 + gathers, CP, G, strip)
+    round3 = begin(12, U3, S.at[2], L.at[2], 3)
     for item in coarse_res:
         item.wait_recv()
 
@@ -300,13 +305,25 @@
                 x = jnp.where(even_wide, pltpu.roll(x, LAT - 1, 1), x)
             EX[c, q + 1, pl.ds(0, wide, 2), :] = x
             EX[c, q + 1, pl.ds(1, wide, 2), :] = x
-    for c in range(3):
-        for r in range(-1, R + 1):
-            U3[c, r + 1] = U2[c, r + 1] + EX[c, r // 2 + 1]
-
-    sweep(U3, U4)
-    round3 = begin(12, U4, S.at[2], L.at[2], 3)
-    finish(round3, U4, L.at[2], 3)
+    finish(round_w, WT, LW, 6)
+    finish(round3, U3, L.at[2], 3)
+    lo, hi = PAD // 2, C + PAD + PAD // 2
+
+    for r in range(-1, R + 1):
+        for c in range(3):
+            x = EX[c, r // 2 + 1, lo:hi, :]
+            xn = [
+                EX[c, r // 2 + 1, lo - 1 : hi - 1, :],
+                EX[c, r // 2 + 1, lo + 1 : hi + 1, :],
+                EX[c, (r - 1) // 2 + 1, lo:hi, :],
+                EX[c, (r + 1) // 2 + 1, lo:hi, :],
+                pltpu.roll(x, 1, 1),
+                pltpu.roll(x, LAT - 1, 1),
+            ]
+            t = U3[c, r + 1, lo:hi, :] + 0.2 * x
+            for k in range(6):
+                t = t + WT[k, r + 1, lo:hi, :] * xn[k]
+            U4[c, r + 1, lo:hi, :] = t
 
     def closing(r, carry):
         for c in range(3):
@@ -336,7 +353,7 @@
         f32 = jnp.float32
         frame = lambda n, rows: pltpu.VMEM((n, rows, wide, LAT), f32)
         block = lambda *dims: pltpu.VMEM(dims + (C, LAT), f32)
-        copies = 16 + 2 * (3 * nj - 1)
+        copies = 20 + 2 * (3 * nj - 1)
         vmem, place = pl.BlockSpec(memory_space=pltpu.VMEM), pl.BlockSpec(memory_space=pl.ANY)
         P8 = half * nj
         results = pl.pallas_call(
@@ -350,7 +367,7 @@
             scratch_shapes=[
                 block(3, R), block(3, R), pltpu.SemaphoreType.DMA((5,)),
                 frame(5, R + 2), frame(3, R + 2), frame(3, R + 2), frame(3, R + 2), frame(3, R + 2),
-                block(6, R), block(3, R), block(R), block(4, 2 * half),
+                pltpu.VMEM((2, 6, R, LAT), f32), pltpu.VMEM((2, 6, R, LAT), f32), frame(6, R + 2), block(3, R), block(R), block(4, 2 * half),
                 pltpu.VMEM((3, half, cols, LAT), f32), pltpu.VMEM((1, half, cols, LAT), f32),
                 frame(3, P8 + 2), frame(1, P8 + 2), block(7, P8), block(3, P8),
                 frame(3, P8 + 2), frame(3, P8 + 2), frame(3, 2 * half + 2),

time: 38.5 us -> 34.7 us (0.901)
  Pallas kernels: 37.7 us -> 34 us
    pallas_call x1, Pallas kernels: 36.9 us -> 33.1 us  [local(): pl.pallas_call(functools.partial(kernel, ni, nj), out_shape=(pltpu.VMEM(a...]
where the time goes in v2:
time: 34.7 us; the launch traced here: 34.6 us
  Pallas kernels  34 us (98%)
  between operations  0.64 us (2%)
    pallas_call x1, Pallas kernels, local(): pl.pallas_call(functools.partial(kernel, ni, nj), out_shape=(pltpu.VMEM(a...  33.1 us
    pallas_call x1, Pallas kernels, local(): pl.pallas_call(deliver, out_shape=(jax.ShapeDtypeStruct(adjoint_temp.shap...  0.81 us

profile of v2, /device:TPU:1, one launch (start us, length us, event | category | flops | bytes accessed | tf_op | source)
XLA Modules:
  0.0 34.6 jit_solution(17258700832987230160)
XLA Ops:
  0.6 33.1 %shard_map.68 = (f32[8,32,128]{2,1,0:T(8,128)S(1)}, f32[3,8,32,128]{3,2,1,0:T(8,128)S(1)}) custom-call(f32[8,32,128]{2,1,0:T(8,128)} %temp_hbm.1, f32[8,32,128]{2,1,0:T(8,128)} %visc_hbm.1, f32[3,8,32,128]{3,2,1,0:T(8,128)} %vel_hbm.1, f32[3,8,32,128]{3,2,1,0:T(8,128)} %mis_hbm.1, f32[3,8,32,128]{3,2,1,0:T(8,128)} %guess_hbm.1), custom_call_target="tpu_custom_call" | custom-call | tf_op jit(solution)/shard_map/pallas_call | solution.py:359
  33.8 0.8 %shard_map.69 = (f32[8,32,128]{2,1,0:T(8,128)}, f32[3,8,32,128]{3,2,1,0:T(8,128)}) custom-call(f32[8,32,128]{2,1,0:T(8,128)S(1)} %get-tuple-element.4.tn_ref, f32[3,8,32,128]{3,2,1,0:T(8,128)S(1)} %get-tuple-element.5.out_ref), custom_call_target="tpu_custom_call" | custom-call | tf_op jit(solution)/shard_map/pallas_call | solution.py:380

commit v3 on v2

--- a/solution.py
+++ b/solution.py
@@ -170,7 +170,7 @@
         B[2, r] = mis_ref[2, r] * inv
         return carry
 
-    lax.fori_loop(0, R, setup, 0)
+    lax.fori_loop(0, R, setup, 0, unroll=True)
 
     @pl.when(j == 0)
     def _():
@@ -194,7 +194,7 @@
                 dst[c, r + 1, PAD : PAD + C, :] = x + t
             return carry
 
-        lax.fori_loop(0, R, body, 0)
+        lax.fori_loop(0, R, body, 0, unroll=True)
 
     sweep(W0, U1)
     round1 = begin(4, U1, S.at[0], L.at[0], 3)
@@ -234,7 +234,7 @@
             CW[6, half * at + r] = 4.0 * inv
         return carry
 
-    lax.fori_loop(0, nj, coarse_setup, 0)
+    lax.fori_loop(0, nj, coarse_setup, 0, unroll=True)
 
     finish(round1, U1, L.at[0], 3)
     sweep(U1, U2)
@@ -250,7 +250,7 @@
             RS[c, q] = D[2 * q] * t + D[2 * q + 1] * s
         return carry
 
-    lax.fori_loop(0, 2 * half, residual, 0)
+    lax.fori_loop(0, 2 * half, residual, 0, unroll=True)
     for c in range(3):
         pack(c, CP.at[c])
     coarse_res = gather(20 + gathers, CP, G, strip)
@@ -265,7 +265,7 @@
             EA[c, p + 1, PAD : PAD + C, :] = b
         return carry
 
-    lax.fori_loop(0, half * nj, coarse_first, 0)
+    lax.fori_loop(0, half * nj, coarse_first, 0, unroll=True)
 
     def coarse_sweep(src, dst, rim):
         near_rim = 2 * rim <= PAD and cols % 8 == 0
@@ -284,7 +284,10 @@
                     dst[c, p + 1, lo : lo + width, :] = t
             return carry
 
-        lax.fori_loop(jnp.maximum(j - reach, 0), jnp.minimum(j + reach + 1, nj), body, 0)
+        if reach > 1:
+            lax.fori_loop(0, nj, body, 0, unroll=True)
+        else:
+            lax.fori_loop(jnp.maximum(j - reach, 0), jnp.minimum(j + reach + 1, nj), body, 0)
 
     src, dst = EA, EB
     for number in range(NC - 1):
@@ -331,7 +334,7 @@
             out_ref[c, r] = x + t
         return carry
 
-    lax.fori_loop(0, R, closing, 0)
+    lax.fori_loop(0, R, closing, 0, unroll=True)
     for item in pending:
         item.wait_send()
 

time: 34.7 us -> 31.6 us (0.911)
  Pallas kernels: 34 us -> 30.9 us
    pallas_call x1, Pallas kernels: 33.1 us -> 30 us  [local(): pl.pallas_call(functools.partial(kernel, ni, nj), out_shape=(pltpu.VMEM(a...]
where the time goes in v3:
time: 31.6 us; the launch traced here: 31.5 us
  Pallas kernels  30.9 us (98%)
  between operations  0.64 us (2%)
    pallas_call x1, Pallas kernels, local(): pl.pallas_call(functools.partial(kernel, ni, nj), out_shape=(pltpu.VMEM(a...  30 us
    pallas_call x1, Pallas kernels, local(): pl.pallas_call(deliver, out_shape=(jax.ShapeDtypeStruct(adjoint_temp.shap...  0.81 us

profile of v3, /device:TPU:1, one launch (start us, length us, event | category | flops | bytes accessed | tf_op | source)
XLA Modules:
  0.0 31.5 jit_solution(1161499230254829473)
XLA Ops:
  0.6 30.0 %shard_map.68 = (f32[8,32,128]{2,1,0:T(8,128)S(1)}, f32[3,8,32,128]{3,2,1,0:T(8,128)S(1)}) custom-call(f32[8,32,128]{2,1,0:T(8,128)} %temp_hbm.1, f32[8,32,128]{2,1,0:T(8,128)} %visc_hbm.1, f32[3,8,32,128]{3,2,1,0:T(8,128)} %vel_hbm.1, f32[3,8,32,128]{3,2,1,0:T(8,128)} %mis_hbm.1, f32[3,8,32,128]{3,2,1,0:T(8,128)} %guess_hbm.1), custom_call_target="tpu_custom_call" | custom-call | tf_op jit(solution)/shard_map/pallas_call | solution.py:362
  30.7 0.8 %shard_map.69 = (f32[8,32,128]{2,1,0:T(8,128)}, f32[3,8,32,128]{3,2,1,0:T(8,128)}) custom-call(f32[8,32,128]{2,1,0:T(8,128)S(1)} %get-tuple-element.4.tn_ref, f32[3,8,32,128]{3,2,1,0:T(8,128)S(1)} %get-tuple-element.5.out_ref), custom_call_target="tpu_custom_call" | custom-call | tf_op jit(solution)/shard_map/pallas_call | solution.py:383
